TPU v7x, 256 devices: a whole 4x4x8 slice. The times are simulated.
256 devices in a mesh: role: 2 (over z_hi), dp: 32 (over x, z_lo, core), mp: 4 (over y).
Axes of the slice: x: 4, y: 4, z: 8 (z_hi: 2, z_lo: 4; z = z_hi * 4 + z_lo), core: 2. Of those that a mesh axis runs over, the one named last changes fastest.
Arguments:
- state: float32 [2, 2, 8, 2048, 512], P('role', None, None, 'dp', 'mp'), may hold values from 0 to 1
- embed: bfloat16 [2, 1024, 4096], P('role', 'dp', 'mp'), may hold values from -0.09375 to 0.09375
- mlp: bfloat16 [2, 2, 1024, 4096], P('role', None, 'dp', 'mp'), may hold values from -0.1875 to 0.1875
- mom_embed: float32 [2, 1024, 4096], P('role', 'dp', 'mp'), may hold values from -6 to 6
- mom_mlp: float32 [2, 2, 1024, 4096], P('role', None, 'dp', 'mp'), may hold values from -6 to 6
Outputs:
- state_out: float32 [2, 8, 2048, 512], P(None, None, 'dp', 'mp')
- embed_out: bfloat16 [2, 1024, 4096], P('role', 'dp', 'mp')
- mlp_out: bfloat16 [2, 2, 1024, 4096], P('role', None, 'dp', 'mp')
- mom_embed_out: float32 [2, 1024, 4096], P('role', 'dp', 'mp')
- mom_mlp_out: float32 [2, 2, 1024, 4096], P('role', None, 'dp', 'mp')
All inputs are finite; a program needn't handle non-finite values.
Results may differ from a plain program's by a relative error of at most 0.0034.
Values may be sent and summed in bfloat16 or wider, within the bound.
A program may use at most 128 MiB of HBM per device.

v0:
```python
import jax
import jax.numpy as jnp
from jax import lax
from jax.sharding import PartitionSpec as P

PATCH = 16
STEPS = 4
SUBSTRATE_DIFFUSION = 0.2
CATALYST_DIFFUSION = 0.1
FEED_RATE = 0.037
KILL_RATE = 0.06
TIME_STEP = 0.8
GELU_FACTOR = 0.7978845608028654
MOMENTUM_DECAY = 0.9
LEARNING_RATE = 0.003


def extended(cells, sides, width):
    for axis, dim in sides:
        count = lax.axis_size(axis)
        head = lax.slice_in_dim(cells, 0, width, axis=dim)
        tail = lax.slice_in_dim(cells, cells.shape[dim] - width, cells.shape[dim], axis=dim)
        cells = jnp.concatenate(
            [
                lax.ppermute(tail, axis, [(i, (i + 1) % count) for i in range(count)]),
                cells,
                lax.ppermute(head, axis, [((i + 1) % count, i) for i in range(count)]),
            ],
            axis=dim,
        )
    return cells


def from_behind(value, axis, steps):
    count = lax.axis_size(axis)
    leading, last = (max(0, -steps), min(count, count - steps))
    return lax.ppermute(value, axis, [(source, source + steps) for source in range(leading, last)])


def in_blocks(x, dim, count):
    before, after = (x.shape[:dim], x.shape[dim + 1 :])
    return jnp.moveaxis(x.reshape(*before, count, -1, *after), dim, 0)


def summed_on_arrival(x, axis, dim):
    count = lax.axis_size(axis)
    tiles = lax.all_to_all(in_blocks(x, dim, count), axis, 0, 0, tiled=True)
    return jnp.sum(tiles, axis=0)


def joined_along(tiles, dim):
    tiles = jnp.moveaxis(tiles, 0, dim)
    shape = tiles.shape
    return tiles.reshape(*shape[:dim], shape[dim] * shape[dim + 1], *shape[dim + 2 :])


def copy_for_each(x, axis):
    copies = jnp.broadcast_to(x, (lax.axis_size(axis), *x.shape))
    return lax.all_to_all(copies, axis, split_axis=0, concat_axis=0, tiled=True)


def gathered_copies(x, axis, dim):
    return joined_along(copy_for_each(x, axis), dim)


def react(padded):
    center = padded[:, :, 1:-1, 1:-1]
    below_plane = jnp.concatenate([center[:, :1], center[:, :-1]], axis=1)
    above_plane = jnp.concatenate([center[:, 1:], center[:, -1:]], axis=1)
    beside = below_plane + above_plane + padded[:, :, :-2, 1:-1] + padded[:, :, 2:, 1:-1]
    beside = beside + padded[:, :, 1:-1, :-2] + padded[:, :, 1:-1, 2:]
    laplace = beside - 6.0 * center
    substrate = center[0]
    catalyst = center[1]
    growth = substrate * catalyst * catalyst
    new_substrate = substrate + TIME_STEP * (
        SUBSTRATE_DIFFUSION * laplace[0] - growth + FEED_RATE * (1.0 - substrate)
    )
    new_catalyst = catalyst + TIME_STEP * (
        CATALYST_DIFFUSION * laplace[1] + growth - (FEED_RATE + KILL_RATE) * catalyst
    )
    return jnp.stack([new_substrate, new_catalyst])


def gelu_slope(preact):
    cubic = 0.044715 * preact * preact * preact
    tangent = jnp.tanh(GELU_FACTOR * (preact + cubic))
    return 0.5 * (1.0 + tangent) + 0.5 * preact * (1.0 - tangent * tangent) * GELU_FACTOR * (
        1.0 + 3.0 * 0.044715 * preact * preact
    )


def to_patches(brick):
    extent = brick.shape
    blocks = brick.reshape(
        extent[0], extent[1], extent[2] // PATCH, PATCH, extent[3] // PATCH, PATCH
    )
    blocks = blocks.transpose(2, 4, 0, 1, 3, 5)
    return blocks.reshape(
        extent[2] // PATCH * (extent[3] // PATCH), extent[0] * extent[1] * PATCH * PATCH
    )


def advance(cells):
    padded = extended(cells, (("dp", 2), ("mp", 3)), STEPS)
    for iteration in range(STEPS):
        padded = react(padded)
    return padded


def shards(state, embed, mlp, mom_embed, mom_mlp):
    group_index = lax.axis_index("role")
    start_cells = state[0]
    start_half = start_cells.astype(jnp.bfloat16)
    arranged = lax.all_to_all(to_patches(start_half), "mp", split_axis=1, concat_axis=0, tiled=True)
    initial_rows = from_behind(arranged, "role", 1)
    stacked = jnp.concatenate([embed[0], mlp[0, 0], mlp[0, 1]], axis=1)
    whole = lax.all_gather(stacked, "dp", axis=0, tiled=True)
    cells = advance(start_cells)
    arrived = from_behind(cells, "role", 1)
    state_out = jnp.where(group_index == 0, cells, arrived)
    final_rows = to_patches(arrived.astype(jnp.bfloat16))
    targets = lax.all_to_all(final_rows, "mp", split_axis=1, concat_axis=0, tiled=True)
    feature_cols = embed.shape[2]
    hidden_cols = mlp.shape[3]
    embed_full = whole[:, :feature_cols]
    up_full = whole[:, feature_cols : feature_cols + hidden_cols]
    down_full = whole[:, feature_cols + hidden_cols :]
    patch_rows = initial_rows.shape[0]
    loss_scale = float(patch_rows * lax.axis_size("dp")) ** (-0.5)
    embedded = summed_on_arrival(
        jnp.dot(initial_rows, embed_full.T, preferred_element_type=jnp.float32), "mp", 0
    )
    recip = lax.rsqrt(jnp.mean(embedded * embedded, axis=1, keepdims=True) + 1e-06)
    normed = gathered_copies((embedded * recip).astype(jnp.bfloat16), "mp", 0)
    hidden_pre = jnp.dot(normed, up_full, preferred_element_type=jnp.float32)
    active = jax.nn.gelu(hidden_pre, approximate=True).astype(jnp.bfloat16)
    branch = summed_on_arrival(
        jnp.dot(active, down_full.T, preferred_element_type=jnp.float32), "mp", 0
    )
    stream = gathered_copies((embedded + branch).astype(jnp.bfloat16), "mp", 0)
    predicted = initial_rows.astype(jnp.float32) + jnp.dot(
        stream, embed_full, preferred_element_type=jnp.float32
    )
    residual_grad = ((predicted - targets.astype(jnp.float32)) * loss_scale).astype(jnp.bfloat16)
    stream_grad = summed_on_arrival(
        jnp.dot(residual_grad, embed_full.T, preferred_element_type=jnp.float32), "mp", 0
    )
    stream_sent = gathered_copies(stream_grad.astype(jnp.bfloat16), "mp", 0)
    hidden_grad = (
        jnp.dot(stream_sent, down_full, preferred_element_type=jnp.float32) * gelu_slope(hidden_pre)
    ).astype(jnp.bfloat16)
    normed_grad = summed_on_arrival(
        jnp.dot(hidden_grad, up_full.T, preferred_element_type=jnp.float32), "mp", 0
    )
    embed_grad = (
        stream_grad
        + recip * normed_grad
        - embedded
        * (recip * recip * recip)
        * jnp.mean(normed_grad * embedded, axis=1, keepdims=True)
    )
    embed_sent = gathered_copies(embed_grad.astype(jnp.bfloat16), "mp", 0)
    up_part = jnp.dot(normed.T, hidden_grad, preferred_element_type=jnp.float32)
    down_part = jnp.dot(stream_sent.T, active, preferred_element_type=jnp.float32)
    first = jnp.dot(stream.T, residual_grad, preferred_element_type=jnp.float32)
    grads = lax.psum_scatter(
        jnp.concatenate(
            [
                first + jnp.dot(embed_sent.T, initial_rows, preferred_element_type=jnp.float32),
                up_part,
                down_part,
            ],
            axis=1,
        ),
        "dp",
        scatter_dimension=0,
        tiled=True,
    )
    mirrored = from_behind(grads, "role", -1)
    grads = jnp.where(group_index == 0, mirrored, grads)
    grad_embed_rows = grads[:, :feature_cols]
    grad_mlp_rows = jnp.stack(
        [
            grads[:, feature_cols : feature_cols + hidden_cols],
            grads[:, feature_cols + hidden_cols :],
        ]
    )
    mom_embed_out = MOMENTUM_DECAY * mom_embed + grad_embed_rows[None]
    mom_mlp_out = MOMENTUM_DECAY * mom_mlp + grad_mlp_rows[None]
    embed_out = (embed.astype(jnp.float32) - LEARNING_RATE * mom_embed_out).astype(jnp.bfloat16)
    mlp_out = (mlp.astype(jnp.float32) - LEARNING_RATE * mom_mlp_out).astype(jnp.bfloat16)
    return (state_out, embed_out, mlp_out, mom_embed_out, mom_mlp_out)


def solution(mesh):
    placed = (
        P("role", None, None, "dp", "mp"),
        P("role", "dp", "mp"),
        P("role", None, "dp", "mp"),
        P("role", "dp", "mp"),
        P("role", None, "dp", "mp"),
    )
    return jax.shard_map(
        shards,
        mesh=mesh,
        in_specs=placed,
        out_specs=(
            P(None, None, "dp", "mp"),
            P("role", "dp", "mp"),
            P("role", None, "dp", "mp"),
            P("role", "dp", "mp"),
            P("role", None, "dp", "mp"),
        ),
        check_vma=False,
    )
```

profile of v0, /device:TPU:24, one launch (start us, length us, event | category | flops | bytes accessed | tf_op | source)
XLA Modules:
  0.0 440.8 jit_solution(15371048117641775478)
XLA Ops:
  8.2 1.5 pad_maximum_fusion.6
  10.1 6.3 %collective-permute-start.1 = (f32[2,8,4,128]{3,1,2,0:T(8,128)S(1)}, f32[2,8,4,128]{3,1,2,0:T(8,128)S(1)}, u32[]{:S(2)}, u32[]{:S(2)}) collective-permute-start(f32[2,8,4,128]{3,1,2,0:T(8,128)S(1)} %get-tuple-element.66), channel_id=1, source_target_pairs={{4,0},{8,4},{12,8},{16,12},{20,16},{24,20},{28,24},{32,28},{36,32}... | collective-permute-start | bytes 98312 | tf_op jit(solution)/shard_map/ppermute | solution.py:27
  16.4 1.6 collective-permute-done.1
  18.0 5.6 %collective-permute-done = f32[2,8,4,128]{3,1,2,0:T(8,128)S(1)} collective-permute-done((f32[2,8,4,128]{3,1,2,0:T(8,128)S(1)}, f32[2,8,4,128]{3,1,2,0:T(8,128)S(1)}, u32[]{:S(2)}, u32[]{:S(2)}) %collective-permute-start) | collective-permute-done | bytes 32800 | tf_op jit(solution)/shard_map/ppermute | solution.py:25
  25.2 2.5 collective-permute-start.2
  27.8 1.4 convert_element_type.57
  29.1 1.9 copy.104
  31.1 3.8 all_to_all.48
  35.6 4.5 %all-to-all-start = ((bf16[32,4,1024]{2,0,1:T(8,128)(2,1)}), bf16[32,4,1024]{2,0,1:T(8,128)(2,1)}, u32[]{:S(2)}, u32[]{:S(2)}) async-start(bf16[32,4,1024]{2,0,1:T(8,128)(2,1)} %copy.89), calls=%async_computation | async-start | bytes 524288 | tf_op jit(solution)/shard_map/all_to_all | solution.py:115
  47.2 1.6 fusion.37
  48.8 6.5 %collective-permute-start.5 = (bf16[128,1024]{1,0:T(8,128)(2,1)}, bf16[128,1024]{1,0:T(8,128)(2,1)S(1)}, u32[]{:S(2)}, u32[]{:S(2)}) collective-permute-start(bf16[128,1024]{1,0:T(8,128)(2,1)} %bitcast.6), channel_id=1, source_target_pairs={{0,128},{1,129},{2,130},{3,131},{4,132},{5,133},{6,134},{7,135},{8... | collective-permute-start | bytes 786440 | tf_op jit(solution)/shard_map/ppermute | solution.py:37
  57.2 3.0 collective-permute-done.5
  60.2 26.3 %all-gather.2.cloned.1.call-done = bf16[1024,3072]{1,0:T(8,128)(2,1)} async-done(((bf16[32,3072]{1,0:T(8,128)(2,1)}), bf16[1024,3072]{1,0:T(8,128)(2,1)}) %all-gather.2.cloned.1.call-update) | async-done | bytes 6291472 | tf_op jit(solution)/shard_map/all_gather | solution.py:118
  86.5 3.2 fusion.12
  89.7 4.5 %all-to-all-start.1 = ((f32[4,32,1024]{2,1,0:T(8,128)}), f32[4,32,1024]{2,1,0:T(8,128)}, u32[]{:S(2)}, u32[]{:S(2)}) async-start(f32[4,32,1024]{2,1,0:T(8,128)} %bitcast.8), calls=%async_computation.1 | async-start | bytes 1048576 | tf_op jit(solution)/shard_map/all_to_all | solution.py:47
  95.8 6.4 %all-to-all-done.1 = f32[4,32,1024]{2,1,0:T(8,128)} async-done(((f32[4,32,1024]{2,1,0:T(8,128)}), f32[4,32,1024]{2,1,0:T(8,128)}, u32[]{:S(2)}, u32[]{:S(2)}) %all-to-all-start.1) | async-done | bytes 524320 | tf_op jit(solution)/shard_map/all_to_all | solution.py:47
  104.3 5.4 %all-to-all-start.2 = ((bf16[4,32,1024]{2,1,0:T(8,128)(2,1)}), bf16[4,32,1024]{2,1,0:T(8,128)(2,1)S(1)}, u32[]{:S(2)}, u32[]{:S(2)}) async-start(bf16[4,32,1024]{2,1,0:T(8,128)(2,1)} %broadcast_in_dim.20), calls=%async_computation.2 | async-start | bytes 524288 | tf_op jit(solution)/shard_map/all_to_all | solution.py:59
  110.1 2.8 collective-permute-start.4
  112.9 1.4 all-to-all-done.2
  114.3 2.1 fusion.6
  116.5 3.4 fusion.2
  119.9 6.2 %all-to-all-start.3 = ((f32[4,32,1024]{2,1,0:T(8,128)}), f32[4,32,1024]{2,1,0:T(8,128)}, u32[]{:S(2)}, u32[]{:S(2)}) async-start(f32[4,32,1024]{2,1,0:T(8,128)} %bitcast.10), calls=%async_computation.3 | async-start | bytes 1048576 | tf_op jit(solution)/shard_map/all_to_all | solution.py:47
  126.8 2.6 reshape.74
  129.4 1.9 copy.90
  131.3 3.8 all_to_all.56
  135.9 4.9 %all-to-all-start.5 = ((bf16[32,4,1024]{2,0,1:T(8,128)(2,1)}), bf16[32,4,1024]{2,0,1:T(8,128)(2,1)S(1)}, u32[]{:S(2)}, u32[]{:S(2)}) async-start(bf16[32,4,1024]{2,0,1:T(8,128)(2,1)} %copy.91), calls=%async_computation.5 | async-start | bytes 524288 | tf_op jit(solution)/shard_map/all_to_all | solution.py:123
  141.9 3.5 all-to-all-done.5
  145.4 9.1 %all_to_all.72 = bf16[4,32,1024]{2,1,0:T(8,128)(2,1)S(1)} all-to-all(bf16[4,32,1024]{2,1,0:T(8,128)(2,1)S(1)} %broadcast_in_dim.21), channel_id=1, replica_groups=mesh['role'=2,'dp'=32,'mp'=4] {'mp'}, dimensions={0} | all-to-all | bytes 524288 | tf_op jit(solution)/shard_map/all_to_all | solution.py:59
  154.5 2.1 fusion.97
  156.6 2.5 fusion.8
  159.2 10.6 %all_to_all.73 = f32[4,32,1024]{2,1,0:T(8,128)S(1)} all-to-all(f32[4,32,1024]{2,1,0:T(8,128)S(1)} %bitcast.82), channel_id=1, replica_groups=mesh['role'=2,'dp'=32,'mp'=4] {'mp'}, dimensions={0} | all-to-all | bytes 1048576 | tf_op jit(solution)/shard_map/all_to_all | solution.py:47
  169.9 9.0 %all_to_all.74 = bf16[4,32,1024]{2,1,0:T(8,128)(2,1)S(1)} all-to-all(bf16[4,32,1024]{2,1,0:T(8,128)(2,1)S(1)} %broadcast_in_dim.22), channel_id=1, replica_groups=mesh['role'=2,'dp'=32,'mp'=4] {'mp'}, dimensions={0} | all-to-all | bytes 524288 | tf_op jit(solution)/shard_map/all_to_all | solution.py:59
  178.9 2.3 fusion.17
  181.2 3.2 fusion.4
  184.4 5.5 %all-to-all-start.8 = ((f32[4,32,1024]{2,1,0:T(8,128)}), f32[4,32,1024]{2,1,0:T(8,128)S(1)}, u32[]{:S(2)}, u32[]{:S(2)}) async-start(f32[4,32,1024]{2,1,0:T(8,128)} %bitcast.81), calls=%async_computation.8 | async-start | bytes 1048576 | tf_op jit(solution)/shard_map/all_to_all | solution.py:47
  189.9 3.7 fusion.121
  193.6 2.8 fusion.112
  197.4 5.0 %all-to-all-start.9 = ((bf16[4,32,1024]{2,1,0:T(8,128)(2,1)}), bf16[4,32,1024]{2,1,0:T(8,128)(2,1)S(1)}, u32[]{:S(2)}, u32[]{:S(2)}) async-start(bf16[4,32,1024]{2,1,0:T(8,128)(2,1)} %broadcast_in_dim.23), calls=%async_computation.9 | async-start | bytes 524288 | tf_op jit(solution)/shard_map/all_to_all | solution.py:59
  202.4 2.8 fusion.122
  205.1 1.8 all-to-all-done.9
  207.0 3.1 convolution_add_fusion
  210.4 1.3 copy-done.1
  211.7 5.6 %pad_maximum_fusion = f32[1024,3072]{0,1:T(8,128)} fusion(f32[1024,1024]{0,1:T(8,128)S(1)} %copy-done, f32[1024,1024]{0,1:T(8,128)S(1)} %copy-done.1, f32[1024,1024]{0,1:T(8,128)S(1)} %convolution_add_fusion), kind=kLoop, calls=%fused_computation | loop fusion | flops 6291456 | bytes 25165824 | tf_op jit(solution)/shard_map/concatenate | solution.py:168
  217.3 12.6 %copy.99 = f32[1024,3072]{1,0:T(8,128)} copy(f32[1024,3072]{0,1:T(8,128)} %pad_maximum_fusion) | data formatting | bytes 25165824
  230.0 183.8 %reduce-scatter.4.cloned.1.call-done = f32[32,3072]{1,0:T(8,128)} async-done(((f32[1024,3072]{1,0:T(8,128)}), f32[32,3072]{1,0:T(8,128)}) %reduce-scatter.4.cloned.1.call-update) | async-done | bytes 393232 | tf_op jit(solution)/shard_map/reduce_scatter | solution.py:167
  413.8 1.3 collective-permute-start.6
  418.7 9.7 %collective-permute-done.6 = f32[32,3072]{1,0:T(8,128)} collective-permute-done((f32[32,3072]{1,0:T(8,128)}, f32[32,3072]{1,0:T(8,128)}, u32[]{:S(2)}, u32[]{:S(2)}) %collective-permute-start.6) | collective-permute-done | bytes 393248 | tf_op jit(solution)/shard_map/ppermute | solution.py:37
  428.3 1.5 copy.93
  (109 shorter events, 28.3 us)
Async XLA Ops:
  7.2 2.5 copy-start.3
  7.2 79.3 %all-gather.2.cloned.1.call-start = ((), (), s32[]{:S(2)}) async-start(), calls=%async_computation.11 | async-start | bytes 6488064 | tf_op jit(solution)/shard_map/all_gather | solution.py:118
  10.1 7.9 %collective-permute-start.1 = (f32[2,8,4,128]{3,1,2,0:T(8,128)S(1)}, f32[2,8,4,128]{3,1,2,0:T(8,128)S(1)}, u32[]{:S(2)}, u32[]{:S(2)}) collective-permute-start(f32[2,8,4,128]{3,1,2,0:T(8,128)S(1)} %get-tuple-element.66), channel_id=1, source_target_pairs={{4,0},{8,4},{12,8},{16,12},{20,16},{24,20},{28,24},{32,28},{36,32}... | collective-permute-start | bytes 98312 | tf_op jit(solution)/shard_map/ppermute | solution.py:27
  16.4 7.2 %collective-permute-start = (f32[2,8,4,128]{3,1,2,0:T(8,128)S(1)}, f32[2,8,4,128]{3,1,2,0:T(8,128)S(1)}, u32[]{:S(2)}, u32[]{:S(2)}) collective-permute-start(f32[2,8,4,128]{3,1,2,0:T(8,128)S(1)} %get-tuple-element.65), channel_id=1, source_target_pairs={{0,4},{4,8},{8,12},{12,16},{16,20},{20,24},{24,28},{28,32},{32,36}... | collective-permute-start | bytes 98312 | tf_op jit(solution)/shard_map/ppermute | solution.py:25
  24.1 16.0 %collective-permute-start.3 = (f32[2,8,72,4]{2,1,3,0:T(8,128)S(1)}, f32[2,8,72,4]{2,1,3,0:T(8,128)S(1)}, u32[]{:S(2)}, u32[]{:S(2)}) collective-permute-start(f32[2,8,72,4]{2,1,3,0:T(8,128)S(1)} %copy.81), channel_id=1, source_target_pairs={{1,0},{2,1},{3,2},{0,3},{5,4},{6,5},{7,6},{4,7},{9,8},{10,9},{11,1... | collective-permute-start | bytes 55304 | tf_op jit(solution)/shard_map/ppermute | solution.py:27
  25.2 15.2 %collective-permute-start.2 = (f32[2,8,72,4]{2,1,3,0:T(8,128)S(1)}, f32[2,8,72,4]{2,1,3,0:T(8,128)S(1)}, u32[]{:S(2)}, u32[]{:S(2)}) collective-permute-start(f32[2,8,72,4]{2,1,3,0:T(8,128)S(1)} %copy.80), channel_id=1, source_target_pairs={{0,1},{1,2},{2,3},{3,0},{4,5},{5,6},{6,7},{7,4},{8,9},{9,10},{10,1... | collective-permute-start | bytes 55304 | tf_op jit(solution)/shard_map/ppermute | solution.py:25
  35.6 13.2 %all-to-all-start = ((bf16[32,4,1024]{2,0,1:T(8,128)(2,1)}), bf16[32,4,1024]{2,0,1:T(8,128)(2,1)}, u32[]{:S(2)}, u32[]{:S(2)}) async-start(bf16[32,4,1024]{2,0,1:T(8,128)(2,1)} %copy.89), calls=%async_computation | async-start | bytes 524288 | tf_op jit(solution)/shard_map/all_to_all | solution.py:115
  48.8 7.2 %copy-start.2 = (f32[2,7,66,130]{3,1,2,0:T(8,128)S(1)}, f32[2,7,66,130]{3,1,2,0:T(8,128)}, u32[]{:S(2)}) copy-start(f32[2,7,66,130]{3,1,2,0:T(8,128)} %get-tuple-element.58) | copy-start | bytes 1441444
  48.8 11.4 %collective-permute-start.5 = (bf16[128,1024]{1,0:T(8,128)(2,1)}, bf16[128,1024]{1,0:T(8,128)(2,1)S(1)}, u32[]{:S(2)}, u32[]{:S(2)}) collective-permute-start(bf16[128,1024]{1,0:T(8,128)(2,1)} %bitcast.6), channel_id=1, source_target_pairs={{0,128},{1,129},{2,130},{3,131},{4,132},{5,133},{6,134},{7,135},{8... | collective-permute-start | bytes 786440 | tf_op jit(solution)/shard_map/ppermute | solution.py:37
  60.2 29.5 %copy-start.12 = (bf16[128,1024]{1,0:T(8,128)(2,1)}, bf16[128,1024]{1,0:T(8,128)(2,1)S(1)}, u32[]{:S(2)}) copy-start(bf16[128,1024]{1,0:T(8,128)(2,1)S(1)} %collective-permute-done.5) | copy-start | bytes 786436
  89.7 12.5 %all-to-all-start.1 = ((f32[4,32,1024]{2,1,0:T(8,128)}), f32[4,32,1024]{2,1,0:T(8,128)}, u32[]{:S(2)}, u32[]{:S(2)}) async-start(f32[4,32,1024]{2,1,0:T(8,128)} %bitcast.8), calls=%async_computation.1 | async-start | bytes 1048576 | tf_op jit(solution)/shard_map/all_to_all | solution.py:47
  104.3 10.1 %all-to-all-start.2 = ((bf16[4,32,1024]{2,1,0:T(8,128)(2,1)}), bf16[4,32,1024]{2,1,0:T(8,128)(2,1)S(1)}, u32[]{:S(2)}, u32[]{:S(2)}) async-start(bf16[4,32,1024]{2,1,0:T(8,128)(2,1)} %broadcast_in_dim.20), calls=%async_computation.2 | async-start | bytes 524288 | tf_op jit(solution)/shard_map/all_to_all | solution.py:59
  110.1 16.0 %collective-permute-start.4 = (f32[2,8,64,128]{3,2,1,0:T(8,128)S(1)}, f32[2,8,64,128]{3,2,1,0:T(8,128)S(1)}, u32[]{:S(2)}, u32[]{:S(2)}) collective-permute-start(f32[2,8,64,128]{3,2,1,0:T(8,128)S(1)} %copy.84), channel_id=1, source_target_pairs={{0,128},{1,129},{2,130},{3,131},{4,132},{5,133},{6,134},{7,135},{8... | collective-permute-start | bytes 1572872 | tf_op jit(solution)/shard_map/ppermute | solution.py:37
  114.3 2.1 copy-start.5
  116.5 3.4 copy-start.8
  119.9 16.0 %all-to-all-start.3 = ((f32[4,32,1024]{2,1,0:T(8,128)}), f32[4,32,1024]{2,1,0:T(8,128)}, u32[]{:S(2)}, u32[]{:S(2)}) async-start(f32[4,32,1024]{2,1,0:T(8,128)} %bitcast.10), calls=%async_computation.3 | async-start | bytes 1048576 | tf_op jit(solution)/shard_map/all_to_all | solution.py:47
  135.9 18.6 %copy-start.13 = (bf16[128,1024]{1,0:T(8,128)(2,1)S(1)}, bf16[128,1024]{1,0:T(8,128)(2,1)}, u32[]{:S(2)}) copy-start(bf16[128,1024]{1,0:T(8,128)(2,1)} %copy-done.12) | copy-start | bytes 786436
  135.9 9.5 %all-to-all-start.5 = ((bf16[32,4,1024]{2,0,1:T(8,128)(2,1)}), bf16[32,4,1024]{2,0,1:T(8,128)(2,1)S(1)}, u32[]{:S(2)}, u32[]{:S(2)}) async-start(bf16[32,4,1024]{2,0,1:T(8,128)(2,1)} %copy.91), calls=%async_computation.5 | async-start | bytes 524288 | tf_op jit(solution)/shard_map/all_to_all | solution.py:123
  156.6 2.5 copy-start.15
  159.1 19.8 %copy-start.9 = (f32[128,1024]{1,0:T(8,128)S(1)}, f32[128,1024]{1,0:T(8,128)}, u32[]{:S(2)}) copy-start(f32[128,1024]{1,0:T(8,128)} %copy-done.8) | copy-start | bytes 1572868
  184.4 12.0 %all-to-all-start.8 = ((f32[4,32,1024]{2,1,0:T(8,128)}), f32[4,32,1024]{2,1,0:T(8,128)S(1)}, u32[]{:S(2)}, u32[]{:S(2)}) async-start(f32[4,32,1024]{2,1,0:T(8,128)} %bitcast.81), calls=%async_computation.8 | async-start | bytes 1048576 | tf_op jit(solution)/shard_map/all_to_all | solution.py:47
  196.4 6.0 %copy-start.6 = (bf16[4,32,1024]{2,1,0:T(8,128)(2,1)S(1)}, bf16[4,32,1024]{2,1,0:T(8,128)(2,1)}, u32[]{:S(2)}) copy-start(bf16[4,32,1024]{2,1,0:T(8,128)(2,1)} %copy-done.5) | copy-start | bytes 786436
  197.4 9.6 %all-to-all-start.9 = ((bf16[4,32,1024]{2,1,0:T(8,128)(2,1)}), bf16[4,32,1024]{2,1,0:T(8,128)(2,1)S(1)}, u32[]{:S(2)}, u32[]{:S(2)}) async-start(bf16[4,32,1024]{2,1,0:T(8,128)(2,1)} %broadcast_in_dim.23), calls=%async_computation.9 | async-start | bytes 524288 | tf_op jit(solution)/shard_map/all_to_all | solution.py:59
  202.4 4.6 %copy-start.14 = (bf16[128,1024]{1,0:T(8,128)(2,1)S(1)}, bf16[128,1024]{1,0:T(8,128)(2,1)}, u32[]{:S(2)}) copy-start(bf16[128,1024]{1,0:T(8,128)(2,1)} %copy-done.12) | copy-start | bytes 786436
  202.4 211.5 %reduce-scatter.4.cloned.1.call-start = ((), (), s32[]{:S(2)}) async-start(), calls=%async_computation.12 | async-start | bytes 12976128 | tf_op jit(solution)/shard_map/reduce_scatter | solution.py:167
  207.0 3.5 copy-start
  207.0 4.7 %copy-start.1 = (f32[1024,1024]{0,1:T(8,128)S(1)}, f32[1024,1024]{0,1:T(8,128)}, u32[]{:S(2)}) copy-start(f32[1024,1024]{0,1:T(8,128)} %fusion.122) | copy-start | bytes 12582916
  230.0 185.1 %copy-start.16 = (bf16[1,32,1024]{2,1,0:T(8,128)(2,1)S(1)}, bf16[1,32,1024]{2,1,0:T(8,128)(2,1)}, u32[]{:S(2)}) copy-start(bf16[1,32,1024]{2,1,0:T(8,128)(2,1)} %param.6) | copy-start | bytes 196612
  230.0 186.0 %copy-start.18 = (f32[1,32,1024]{2,1,0:T(8,128)S(1)}, f32[1,32,1024]{2,1,0:T(8,128)}, u32[]{:S(2)}) copy-start(f32[1,32,1024]{2,1,0:T(8,128)} %param.8) | copy-start | bytes 393220
  413.8 14.5 %collective-permute-start.6 = (f32[32,3072]{1,0:T(8,128)}, f32[32,3072]{1,0:T(8,128)}, u32[]{:S(2)}, u32[]{:S(2)}) collective-permute-start(f32[32,3072]{1,0:T(8,128)} %reduce-scatter.4.cloned.1.call-done), channel_id=1, source_target_pairs={{128,0},{129,1},{130,2},{131,3},{132,4},{133,5},{134,6},{135,7},{1... | collective-permute-start | bytes 1179656 | tf_op jit(solution)/shard_map/ppermute | solution.py:37
  417.0 1.2 copy-start.11
  430.0 1.0 copy-start.4
  430.0 1.1 copy-start.7
  431.2 2.0 copy-start.10
  431.2 2.0 copy-start.17
Sparse Core Ops, SparseCore 0:
  10.4 76.0 all-gather.1
  230.1 183.6 reduce-scatter.3
where the time goes:
time: 442 us; the launch traced here: 441 us
  waiting for transfers between devices  243 us (55%)
  starting transfers between devices  56.4 us (13%)
  local copies, waits for them, and re-layouts  44.3 us (10%)
  matrix products  31.1 us (7%)
  blocking collectives  28.7 us (6%)
  other arithmetic  22.5 us (5%)
  between operations  14.5 us (3%)
    reduce_scatter x1, waiting for transfers between devices, shards(): lax.psum_scatter(jnp.concatenate([first + jnp.dot(embed_sent.T, initial_r...  184 us
    all_gather x1, waiting for transfers between devices, shards(): whole = lax.all_gather(stacked, 'dp', axis=0, tiled=True)  26.3 us
    unnamed x46, local copies, waits for them, and re-layouts  20.4 us
    all_to_all x2, blocking collectives, copy_for_each(): return lax.all_to_all(copies, axis, split_axis=0, concat_axis=0, tiled=True)  18.1 us
    all_to_all x3, starting transfers between devices, summed_on_arrival(): tiles = lax.all_to_all(in_blocks(x, dim, count), axis, 0, 0, tiled=True)  16.2 us
    ppermute x3, waiting for transfers between devices, from_behind(): lax.ppermute(value, axis, [(source, source + steps) for source in range(l...  12.7 us
    all_to_all x1, blocking collectives, summed_on_arrival(): tiles = lax.all_to_all(in_blocks(x, dim, count), axis, 0, 0, tiled=True)  10.6 us
    ppermute x3, starting transfers between devices, from_behind(): lax.ppermute(value, axis, [(source, source + steps) for source in range(l...  10.6 us
  transfers between devices with their start and end apart: 16, of which 10 were waited for; matrix products, arithmetic and copies ran while one was open for 10% of the time, Pallas kernels for 0%

commit v1 on v0

--- a/solution.py
+++ b/solution.py
@@ -115,7 +115,8 @@
     arranged = lax.all_to_all(to_patches(start_half), "mp", split_axis=1, concat_axis=0, tiled=True)
     initial_rows = from_behind(arranged, "role", 1)
     stacked = jnp.concatenate([embed[0], mlp[0, 0], mlp[0, 1]], axis=1)
-    whole = lax.all_gather(stacked, "dp", axis=0, tiled=True)
+    sent = jnp.stack([stacked] * lax.axis_size("dp"))
+    whole = jnp.concatenate(lax.all_to_all(sent, "dp", 0, 0), axis=0)
     cells = advance(start_cells)
     arrived = from_behind(cells, "role", 1)
     state_out = jnp.where(group_index == 0, cells, arrived)

time: 442 us -> 560 us (1.27)
  waiting for transfers between devices: 243 us -> 348 us
  starting transfers between devices: 56.4 us -> 67.9 us
    ppermute x2, waiting for transfers between devices: 1.6 us -> 99.8 us  [extended(): lax.ppermute(head, axis, [((i + 1) % count, i) for i in range(count)])]
    all_gather x1 -> x0, waiting for transfers between devices: 26.3 us -> none  [shards(): whole = lax.all_gather(stacked, 'dp', axis=0, tiled=True)]
    reduce_scatter x1, waiting for transfers between devices: 184 us -> 203 us  [shards(): lax.psum_scatter(jnp.concatenate([first + jnp.dot(embed_sent.T, initial_r...]
    all_to_all x0 -> x1, waiting for transfers between devices: none -> 13.6 us  [shards(): whole = jnp.concatenate(lax.all_to_all(sent, 'dp', 0, 0), axis=0)]
    all_to_all x0 -> x1, starting transfers between devices: none -> 7.75 us  [shards(): whole = jnp.concatenate(lax.all_to_all(sent, 'dp', 0, 0), axis=0)]
    unnamed x46 -> x40, local copies, waits for them, and re-layouts: 20.4 us -> 20.4 us
  transfers between devices with their start and end apart: 16 -> 16, of which waited for: 10 -> 12; matrix products, arithmetic and copies ran while one was open for 10% -> 7% of each run, Pallas kernels for 0% -> 0%
where the time goes in v1:
time: 560 us; the launch traced here: 558 us
  waiting for transfers between devices  348 us (62%)
  starting transfers between devices  67.9 us (12%)
  local copies, waits for them, and re-layouts  46.8 us (8%)
  matrix products  31.2 us (6%)
  blocking collectives  28.9 us (5%)
  other arithmetic  21 us (4%)
  between operations  14.5 us (3%)
    reduce_scatter x1, waiting for transfers between devices, shards(): lax.psum_scatter(jnp.concatenate([first + jnp.dot(embed_sent.T, initial_r...  203 us
    ppermute x2, waiting for transfers between devices, extended(): lax.ppermute(head, axis, [((i + 1) % count, i) for i in range(count)])  99.8 us
    unnamed x40, local copies, waits for them, and re-layouts  20.4 us
    all_to_all x2, blocking collectives, copy_for_each(): return lax.all_to_all(copies, axis, split_axis=0, concat_axis=0, tiled=True)  18.1 us
    all_to_all x3, starting transfers between devices, summed_on_arrival(): tiles = lax.all_to_all(in_blocks(x, dim, count), axis, 0, 0, tiled=True)  17.9 us
    all_to_all x1, waiting for transfers between devices, shards(): whole = jnp.concatenate(lax.all_to_all(sent, 'dp', 0, 0), axis=0)  13.6 us
    ppermute x3, starting transfers between devices, from_behind(): lax.ppermute(value, axis, [(source, source + steps) for source in range(l...  12 us
  transfers between devices with their start and end apart: 16, of which 12 were waited for; matrix products, arithmetic and copies ran while one was open for 7% of the time, Pallas kernels for 0%

profile of v1, /device:TPU:24, one launch (start us, length us, event | category | flops | bytes accessed | tf_op | source)
XLA Modules:
  0.0 558.1 jit_solution(16478340711368141383)
XLA Ops:
  8.3 1.4 convert_element_type.57
  9.6 1.9 copy.104
  11.5 3.8 all_to_all.52
  16.1 5.9 %all-to-all-start.1 = ((bf16[32,4,1024]{2,0,1:T(8,128)(2,1)}), bf16[32,4,1024]{2,0,1:T(8,128)(2,1)}, u32[]{:S(2)}, u32[]{:S(2)}) async-start(bf16[32,4,1024]{2,0,1:T(8,128)(2,1)} %copy.89), calls=%async_computation.1 | async-start | bytes 524288 | tf_op jit(solution)/shard_map/all_to_all | solution.py:115
  22.1 4.7 all-to-all-done.1
  26.8 3.4 stack.20
  30.2 7.8 %all-to-all-start = ((bf16[32,32,3072]{2,1,0:T(8,128)(2,1)}), bf16[32,32,3072]{2,1,0:T(8,128)(2,1)}, u32[]{:S(2)}, u32[]{:S(2)}) async-start(bf16[32,32,3072]{2,1,0:T(8,128)(2,1)} %stack.20), calls=%async_computation | async-start | bytes 12582912 | tf_op jit(solution)/shard_map/all_to_all | solution.py:119
  38.3 5.5 collective-permute-start.1
  43.8 98.4 %collective-permute-done.1 = f32[2,8,4,128]{3,1,2,0:T(8,128)S(1)} collective-permute-done((f32[2,8,4,128]{3,1,2,0:T(8,128)S(1)}, f32[2,8,4,128]{3,1,2,0:T(8,128)S(1)}, u32[]{:S(2)}, u32[]{:S(2)}) %collective-permute-start.1) | collective-permute-done | bytes 32800 | tf_op jit(solution)/shard_map/ppermute | solution.py:27
  142.2 4.3 collective-permute-done
  147.4 3.4 collective-permute-start.2
  150.8 1.4 collective-permute-done.3
  160.0 7.1 %collective-permute-start.5 = (bf16[128,1024]{1,0:T(8,128)(2,1)}, bf16[128,1024]{1,0:T(8,128)(2,1)}, u32[]{:S(2)}, u32[]{:S(2)}) collective-permute-start(bf16[128,1024]{1,0:T(8,128)(2,1)} %bitcast.7), channel_id=1, source_target_pairs={{0,128},{1,129},{2,130},{3,131},{4,132},{5,133},{6,134},{7,135},{8... | collective-permute-start | bytes 786440 | tf_op jit(solution)/shard_map/ppermute | solution.py:37
  168.9 1.7 collective-permute-done.5
  170.6 13.6 %all-to-all-done = bf16[32,32,3072]{2,1,0:T(8,128)(2,1)} async-done(((bf16[32,32,3072]{2,1,0:T(8,128)(2,1)}), bf16[32,32,3072]{2,1,0:T(8,128)(2,1)}, u32[]{:S(2)}, u32[]{:S(2)}) %all-to-all-start) | async-done | bytes 6291488 | tf_op jit(solution)/shard_map/all_to_all | solution.py:119
  184.1 3.2 fusion.12
  187.4 6.2 %all-to-all-start.2 = ((f32[4,32,1024]{2,1,0:T(8,128)}), f32[4,32,1024]{2,1,0:T(8,128)}, u32[]{:S(2)}, u32[]{:S(2)}) async-start(f32[4,32,1024]{2,1,0:T(8,128)} %bitcast.9), calls=%async_computation.2 | async-start | bytes 1048576 | tf_op jit(solution)/shard_map/all_to_all | solution.py:47
  195.1 5.8 %all-to-all-done.2 = f32[4,32,1024]{2,1,0:T(8,128)} async-done(((f32[4,32,1024]{2,1,0:T(8,128)}), f32[4,32,1024]{2,1,0:T(8,128)}, u32[]{:S(2)}, u32[]{:S(2)}) %all-to-all-start.2) | async-done | bytes 524320 | tf_op jit(solution)/shard_map/all_to_all | solution.py:47
  202.9 5.4 all-to-all-start.3
  208.7 3.6 collective-permute-start.4
  213.0 2.1 fusion.6
  215.1 3.4 fusion.2
  218.5 6.2 %all-to-all-start.4 = ((f32[4,32,1024]{2,1,0:T(8,128)}), f32[4,32,1024]{2,1,0:T(8,128)}, u32[]{:S(2)}, u32[]{:S(2)}) async-start(f32[4,32,1024]{2,1,0:T(8,128)} %bitcast.11), calls=%async_computation.4 | async-start | bytes 1048576 | tf_op jit(solution)/shard_map/all_to_all | solution.py:47
  225.5 2.6 reshape.80
  228.0 1.9 copy.90
  230.0 3.8 all_to_all.60
  234.5 4.8 all-to-all-start.6
  240.4 3.5 all-to-all-done.6
  243.9 9.1 %all_to_all.77 = bf16[4,32,1024]{2,1,0:T(8,128)(2,1)S(1)} all-to-all(bf16[4,32,1024]{2,1,0:T(8,128)(2,1)S(1)} %broadcast_in_dim.21), channel_id=1, replica_groups=mesh['role'=2,'dp'=32,'mp'=4] {'mp'}, dimensions={0} | all-to-all | bytes 524288 | tf_op jit(solution)/shard_map/all_to_all | solution.py:59
  253.0 2.1 fusion.97
  255.1 2.5 fusion.8
  257.7 10.8 %all_to_all.78 = f32[4,32,1024]{2,1,0:T(8,128)S(1)} all-to-all(f32[4,32,1024]{2,1,0:T(8,128)S(1)} %bitcast.83), channel_id=1, replica_groups=mesh['role'=2,'dp'=32,'mp'=4] {'mp'}, dimensions={0} | all-to-all | bytes 1048576 | tf_op jit(solution)/shard_map/all_to_all | solution.py:47
  268.5 9.1 %all_to_all.79 = bf16[4,32,1024]{2,1,0:T(8,128)(2,1)S(1)} all-to-all(bf16[4,32,1024]{2,1,0:T(8,128)(2,1)S(1)} %broadcast_in_dim.22), channel_id=1, replica_groups=mesh['role'=2,'dp'=32,'mp'=4] {'mp'}, dimensions={0} | all-to-all | bytes 524288 | tf_op jit(solution)/shard_map/all_to_all | solution.py:59
  277.6 2.3 fusion.17
  279.8 3.2 fusion.4
  283.0 5.5 all-to-all-start.9
  288.5 3.7 fusion.121
  292.3 2.8 fusion.112
  296.0 5.1 all-to-all-start.10
  301.1 2.8 fusion.122
  303.9 1.8 all-to-all-done.10
  305.7 3.2 convolution_add_fusion
  310.5 5.6 %pad_maximum_fusion = f32[1024,3072]{0,1:T(8,128)} fusion(f32[1024,1024]{0,1:T(8,128)S(1)} %copy-done, f32[1024,1024]{0,1:T(8,128)S(1)} %copy-done.1, f32[1024,1024]{0,1:T(8,128)S(1)} %convolution_add_fusion), kind=kLoop, calls=%fused_computation | loop fusion | flops 6291456 | bytes 25165824 | tf_op jit(solution)/shard_map/concatenate | solution.py:169
  316.1 12.6 %copy.99 = f32[1024,3072]{1,0:T(8,128)} copy(f32[1024,3072]{0,1:T(8,128)} %pad_maximum_fusion) | data formatting | bytes 25165824
  328.8 202.8 %reduce-scatter.4.cloned.1.call-done = f32[32,3072]{1,0:T(8,128)} async-done(((f32[1024,3072]{1,0:T(8,128)}), f32[32,3072]{1,0:T(8,128)}) %reduce-scatter.4.cloned.1.call-update) | async-done | bytes 393232 | tf_op jit(solution)/shard_map/reduce_scatter | solution.py:168
  531.6 1.3 collective-permute-start.6
  536.5 9.1 %collective-permute-done.6 = f32[32,3072]{1,0:T(8,128)} collective-permute-done((f32[32,3072]{1,0:T(8,128)}, f32[32,3072]{1,0:T(8,128)}, u32[]{:S(2)}, u32[]{:S(2)}) %collective-permute-start.6) | collective-permute-done | bytes 393248 | tf_op jit(solution)/shard_map/ppermute | solution.py:37
  545.6 1.5 copy.93
  (103 shorter events, 30.1 us)
Async XLA Ops:
  11.5 10.5 %copy-start.9 = (bf16[1,2,32,1024]{3,2,1,0:T(8,128)(2,1)S(1)}, bf16[1,2,32,1024]{3,2,1,0:T(8,128)(2,1)}, u32[]{:S(2)}) copy-start(bf16[1,2,32,1024]{3,2,1,0:T(8,128)(2,1)} %param.7) | copy-start | bytes 393220
  15.3 6.7 %copy-start.12 = (bf16[1,32,1024]{2,1,0:T(8,128)(2,1)S(1)}, bf16[1,32,1024]{2,1,0:T(8,128)(2,1)}, u32[]{:S(2)}) copy-start(bf16[1,32,1024]{2,1,0:T(8,128)(2,1)} %param.6) | copy-start | bytes 196612
  16.1 10.6 %all-to-all-start.1 = ((bf16[32,4,1024]{2,0,1:T(8,128)(2,1)}), bf16[32,4,1024]{2,0,1:T(8,128)(2,1)}, u32[]{:S(2)}, u32[]{:S(2)}) async-start(bf16[32,4,1024]{2,0,1:T(8,128)(2,1)} %copy.89), calls=%async_computation.1 | async-start | bytes 524288 | tf_op jit(solution)/shard_map/all_to_all | solution.py:115
  30.2 7.8 %copy-start.2 = (f32[1,2,8,64,128]{4,3,2,1,0:T(8,128)S(1)}, f32[1,2,8,64,128]{4,3,2,1,0:T(8,128)}, u32[]{:S(2)}) copy-start(f32[1,2,8,64,128]{4,3,2,1,0:T(8,128)} %param.5) | copy-start | bytes 1572868
  30.2 154.0 %all-to-all-start = ((bf16[32,32,3072]{2,1,0:T(8,128)(2,1)}), bf16[32,32,3072]{2,1,0:T(8,128)(2,1)}, u32[]{:S(2)}, u32[]{:S(2)}) async-start(bf16[32,32,3072]{2,1,0:T(8,128)(2,1)} %stack.20), calls=%async_computation | async-start | bytes 12582912 | tf_op jit(solution)/shard_map/all_to_all | solution.py:119
  38.3 103.9 %collective-permute-start.1 = (f32[2,8,4,128]{3,1,2,0:T(8,128)S(1)}, f32[2,8,4,128]{3,1,2,0:T(8,128)S(1)}, u32[]{:S(2)}, u32[]{:S(2)}) collective-permute-start(f32[2,8,4,128]{3,1,2,0:T(8,128)S(1)} %get-tuple-element.66), channel_id=1, source_target_pairs={{4,0},{8,4},{12,8},{16,12},{20,16},{24,20},{28,24},{32,28},{36,32}... | collective-permute-start | bytes 98312 | tf_op jit(solution)/shard_map/ppermute | solution.py:27
  43.8 102.7 %collective-permute-start = (f32[2,8,4,128]{3,1,2,0:T(8,128)S(1)}, f32[2,8,4,128]{3,1,2,0:T(8,128)S(1)}, u32[]{:S(2)}, u32[]{:S(2)}) collective-permute-start(f32[2,8,4,128]{3,1,2,0:T(8,128)S(1)} %get-tuple-element.65), channel_id=1, source_target_pairs={{0,4},{4,8},{8,12},{12,16},{16,20},{20,24},{24,28},{28,32},{32,36}... | collective-permute-start | bytes 98312 | tf_op jit(solution)/shard_map/ppermute | solution.py:25
  147.1 5.2 collective-permute-start.3
  147.4 5.2 collective-permute-start.2
  160.0 10.6 %collective-permute-start.5 = (bf16[128,1024]{1,0:T(8,128)(2,1)}, bf16[128,1024]{1,0:T(8,128)(2,1)}, u32[]{:S(2)}, u32[]{:S(2)}) collective-permute-start(bf16[128,1024]{1,0:T(8,128)(2,1)} %bitcast.7), channel_id=1, source_target_pairs={{0,128},{1,129},{2,130},{3,131},{4,132},{5,133},{6,134},{7,135},{8... | collective-permute-start | bytes 786440 | tf_op jit(solution)/shard_map/ppermute | solution.py:37
  187.4 13.5 %all-to-all-start.2 = ((f32[4,32,1024]{2,1,0:T(8,128)}), f32[4,32,1024]{2,1,0:T(8,128)}, u32[]{:S(2)}, u32[]{:S(2)}) async-start(f32[4,32,1024]{2,1,0:T(8,128)} %bitcast.9), calls=%async_computation.2 | async-start | bytes 1048576 | tf_op jit(solution)/shard_map/all_to_all | solution.py:47
  202.9 10.1 %all-to-all-start.3 = ((bf16[4,32,1024]{2,1,0:T(8,128)(2,1)}), bf16[4,32,1024]{2,1,0:T(8,128)(2,1)S(1)}, u32[]{:S(2)}, u32[]{:S(2)}) async-start(bf16[4,32,1024]{2,1,0:T(8,128)(2,1)} %broadcast_in_dim.20), calls=%async_computation.3 | async-start | bytes 524288 | tf_op jit(solution)/shard_map/all_to_all | solution.py:59
  208.7 16.0 %collective-permute-start.4 = (f32[2,8,64,128]{3,2,1,0:T(8,128)S(1)}, f32[2,8,64,128]{3,2,1,0:T(8,128)S(1)}, u32[]{:S(2)}, u32[]{:S(2)}) collective-permute-start(f32[2,8,64,128]{3,2,1,0:T(8,128)S(1)} %copy.84), channel_id=1, source_target_pairs={{0,128},{1,129},{2,130},{3,131},{4,132},{5,133},{6,134},{7,135},{8... | collective-permute-start | bytes 1572872 | tf_op jit(solution)/shard_map/ppermute | solution.py:37
  213.0 2.1 copy-start.4
  215.1 3.4 copy-start.7
  218.5 16.0 %all-to-all-start.4 = ((f32[4,32,1024]{2,1,0:T(8,128)}), f32[4,32,1024]{2,1,0:T(8,128)}, u32[]{:S(2)}, u32[]{:S(2)}) async-start(f32[4,32,1024]{2,1,0:T(8,128)} %bitcast.11), calls=%async_computation.4 | async-start | bytes 1048576 | tf_op jit(solution)/shard_map/all_to_all | solution.py:47
  234.5 9.4 %all-to-all-start.6 = ((bf16[32,4,1024]{2,0,1:T(8,128)(2,1)}), bf16[32,4,1024]{2,0,1:T(8,128)(2,1)S(1)}, u32[]{:S(2)}, u32[]{:S(2)}) async-start(bf16[32,4,1024]{2,0,1:T(8,128)(2,1)} %copy.91), calls=%async_computation.6 | async-start | bytes 524288 | tf_op jit(solution)/shard_map/all_to_all | solution.py:124
  255.1 2.5 copy-start.11
  257.6 19.9 %copy-start.8 = (f32[128,1024]{1,0:T(8,128)S(1)}, f32[128,1024]{1,0:T(8,128)}, u32[]{:S(2)}) copy-start(f32[128,1024]{1,0:T(8,128)} %copy-done.7) | copy-start | bytes 1572868
  283.0 12.0 %all-to-all-start.9 = ((f32[4,32,1024]{2,1,0:T(8,128)}), f32[4,32,1024]{2,1,0:T(8,128)S(1)}, u32[]{:S(2)}, u32[]{:S(2)}) async-start(f32[4,32,1024]{2,1,0:T(8,128)} %bitcast.82), calls=%async_computation.9 | async-start | bytes 1048576 | tf_op jit(solution)/shard_map/all_to_all | solution.py:47
  295.0 6.1 %copy-start.5 = (bf16[4,32,1024]{2,1,0:T(8,128)(2,1)S(1)}, bf16[4,32,1024]{2,1,0:T(8,128)(2,1)}, u32[]{:S(2)}) copy-start(bf16[4,32,1024]{2,1,0:T(8,128)(2,1)} %copy-done.4) | copy-start | bytes 786436
  296.0 9.7 %all-to-all-start.10 = ((bf16[4,32,1024]{2,1,0:T(8,128)(2,1)}), bf16[4,32,1024]{2,1,0:T(8,128)(2,1)S(1)}, u32[]{:S(2)}, u32[]{:S(2)}) async-start(bf16[4,32,1024]{2,1,0:T(8,128)(2,1)} %broadcast_in_dim.23), calls=%async_computation.10 | async-start | bytes 524288 | tf_op jit(solution)/shard_map/all_to_all | solution.py:59
  301.1 230.5 %reduce-scatter.4.cloned.1.call-start = ((), (), s32[]{:S(2)}) async-start(), calls=%async_computation.12 | async-start | bytes 12976128 | tf_op jit(solution)/shard_map/reduce_scatter | solution.py:168
  305.7 3.5 copy-start
  305.7 4.8 copy-start.1
  328.8 204.2 %copy-start.13 = (bf16[1,32,1024]{2,1,0:T(8,128)(2,1)S(1)}, bf16[1,32,1024]{2,1,0:T(8,128)(2,1)}, u32[]{:S(2)}) copy-start(bf16[1,32,1024]{2,1,0:T(8,128)(2,1)} %param.6) | copy-start | bytes 196612
  328.8 205.0 %copy-start.15 = (f32[1,32,1024]{2,1,0:T(8,128)S(1)}, f32[1,32,1024]{2,1,0:T(8,128)}, u32[]{:S(2)}) copy-start(f32[1,32,1024]{2,1,0:T(8,128)} %param.8) | copy-start | bytes 393220
  531.6 14.0 %collective-permute-start.6 = (f32[32,3072]{1,0:T(8,128)}, f32[32,3072]{1,0:T(8,128)}, u32[]{:S(2)}, u32[]{:S(2)}) collective-permute-start(f32[32,3072]{1,0:T(8,128)} %reduce-scatter.4.cloned.1.call-done), channel_id=1, source_target_pairs={{128,0},{129,1},{130,2},{131,3},{132,4},{133,5},{134,6},{135,7},{1... | collective-permute-start | bytes 1179656 | tf_op jit(solution)/shard_map/ppermute | solution.py:37
  534.8 1.2 copy-start.10
  547.2 1.0 copy-start.3
  547.3 1.1 copy-start.6
  548.5 2.0 copy-start.14
Sparse Core Ops, SparseCore 0:
  328.9 202.6 reduce-scatter.3
